TPU v7x, 32 devices: a whole 2x2x4 slice. The times are simulated.
32 devices in a mesh: ctx: 4 (over z), head: 4 (over y, x), seg: 2 (over core).
Axes of the slice: x: 2, y: 2, z: 4, core: 2. Of those that a mesh axis runs over, the one named last changes fastest.
Arguments:
- tokens_x: bfloat16 [4096, 2560], P(('ctx', 'seg'), 'head'), may hold values from -6 to 6
- gate_weight: bfloat16 [64, 3, 2560], P(None, None, 'head'), may hold values from -0.15625 to 0.15625
- queries: bfloat16 [4096, 64, 192], P(('ctx', 'seg'), 'head'), may hold values from -48 to 48
- keys: bfloat16 [4096, 4, 192], P(('ctx', 'seg'), 'head'), may hold values from -7 to 7
- values: bfloat16 [4096, 4, 128], P(('ctx', 'seg'), 'head'), may hold values from -24 to 24
- comp_key_weight: bfloat16 [4, 32, 192], P('head'), may hold values from -1 to 1
- comp_value_weight: bfloat16 [4, 32, 128], P('head'), may hold values from -1 to 1
- selected: int32 [32, 4, 16], P(('ctx', 'seg'), 'head'), may hold values from -1 to 63, as said below
Outputs:
- attention: bfloat16 [4096, 64, 128], P(('ctx', 'seg'), 'head')
Inputs may be any that keep to these rules, and one draw needn't show every extreme that they name: Each list names the tile's own fine blocks and block 0, then further blocks; live entries are distinct and at most the tile's last fine block; -1 marks an empty entry. For the tiles of one device (one block of 512 tokens) and one group, the blocks selected from the segment of 512 tokens of any other device number at most 1, and some device reaches it.
All inputs are finite; a program needn't handle non-finite values.
Results may differ from a plain program's by a relative error of at most 0.0059.
Values may be sent and summed in bfloat16 or wider, within the bound.
A program may use at most 128 MiB of HBM per device.

v0:
```python
import jax
import jax.numpy as jnp
from jax import lax
from jax.sharding import PartitionSpec as P

TILE = 128
BLK_S = 64
BLK_C = 32
NSEL = 16
WINDOW = 512


def shifted(value, axis, steps):
    count = lax.axis_size(axis)
    leading, last = (max(0, -steps), min(count, count - steps))
    return lax.ppermute(value, axis, [(source, source + steps) for source in range(leading, last)])


def attend(query, keys_part, values_part, allowed):
    scores = jnp.einsum(
        "rhd,kd->hrk", query, keys_part, preferred_element_type=jnp.float32
    ) * keys_part.shape[-1] ** (-0.5)
    scores = jnp.where(allowed[None], scores, -1e30)
    highest = jnp.max(scores, axis=-1, keepdims=True)
    weights = jnp.where(allowed[None], jnp.exp(scores - highest), 0.0)
    total = jnp.sum(weights, axis=-1)
    rounded = weights.astype(jnp.bfloat16)
    summed = jnp.einsum("hrk,kv->rhv", rounded, values_part, preferred_element_type=jnp.float32)
    return summed / jnp.maximum(total, 1.0).T[:, :, None]


def on_device(
    tokens_x, gate_weight, queries, keys, values, comp_key_weight, comp_value_weight, selected
):
    local_count = queries.shape[0]
    head_count = queries.shape[1]
    key_width = keys.shape[2]
    place = lax.axis_index(("ctx", "seg"))
    offset = place * local_count
    rows = gate_weight
    gates = jax.nn.sigmoid(
        lax.psum_scatter(
            jnp.einsum("hcd,td->hct", rows, tokens_x, preferred_element_type=jnp.float32),
            "head",
            scatter_dimension=0,
            tiled=True,
        )
    )
    own_keys = keys[:, 0]
    own_values = values[:, 0]
    packed = jnp.concatenate([own_keys, own_values], axis=1)
    coarse_local = local_count // BLK_C
    squeezed_keys = jnp.sum(
        own_keys.astype(jnp.float32).reshape(coarse_local, BLK_C, key_width)
        * comp_key_weight[0].astype(jnp.float32)[None],
        axis=1,
    )
    squeezed_values = jnp.sum(
        own_values.astype(jnp.float32).reshape(coarse_local, BLK_C, -1)
        * comp_value_weight[0].astype(jnp.float32)[None],
        axis=1,
    )
    coarse_packed = jnp.concatenate(
        [squeezed_keys.astype(jnp.bfloat16), squeezed_values.astype(jnp.bfloat16)], axis=1
    )
    coarse = lax.all_gather(coarse_packed, ("ctx", "seg"), axis=0, tiled=True)
    coarse_end = jnp.arange(coarse.shape[0], dtype=jnp.int32) * BLK_C + BLK_C - 1
    previous = shifted(packed, ("ctx", "seg"), 1)
    extended = jnp.concatenate([previous, packed], axis=0)
    chosen_all = selected[:, 0, :]
    blocks_all = jnp.maximum(chosen_all, 0)
    everything = lax.all_gather(packed, ("ctx", "seg"), axis=0, tiled=True)
    picked = everything.reshape(-1, BLK_S, packed.shape[1])[blocks_all]

    def one_tile(tile):
        begin = tile * TILE
        rows = offset + begin + jnp.arange(TILE, dtype=jnp.int32)
        query = lax.dynamic_slice_in_dim(queries, begin, TILE, 0)
        gate = lax.dynamic_slice_in_dim(gates, begin, TILE, 2)
        near = lax.dynamic_slice_in_dim(extended, begin + local_count - WINDOW, WINDOW + TILE, 0)
        near_pos = offset + begin - WINDOW + jnp.arange(WINDOW + TILE, dtype=jnp.int32)
        near_ok = (
            (near_pos[None, :] >= 0)
            & (near_pos[None, :] <= rows[:, None])
            & (near_pos[None, :] > rows[:, None] - WINDOW)
        )
        coarse_ok = coarse_end[None, :] <= rows[:, None]
        chosen = chosen_all[tile]
        blocks = jnp.maximum(chosen, 0)
        fine = picked[tile].reshape(NSEL * BLK_S, packed.shape[1])
        fine_pos = (blocks[:, None] * BLK_S + jnp.arange(BLK_S, dtype=jnp.int32)[None, :]).reshape(
            -1
        )
        live = jnp.repeat(chosen >= 0, BLK_S)
        fine_ok = live[None, :] & (fine_pos[None, :] <= rows[:, None])
        coarse_out = attend(query, coarse[:, :key_width], coarse[:, key_width:], coarse_ok)
        fine_out = attend(query, fine[:, :key_width], fine[:, key_width:], fine_ok)
        window_out = attend(query, near[:, :key_width], near[:, key_width:], near_ok)
        mixed = gate[:, 0, :].T[:, :, None] * coarse_out + gate[:, 1, :].T[:, :, None] * fine_out
        mixed = mixed + gate[:, 2, :].T[:, :, None] * window_out
        return mixed.astype(jnp.bfloat16)

    tiles = lax.map(one_tile, jnp.arange(local_count // TILE, dtype=jnp.int32))
    return tiles.reshape(local_count, head_count, -1)


def solution(mesh):
    in_specs = (
        P(("ctx", "seg"), "head"),
        P(None, None, "head"),
        P(("ctx", "seg"), "head", None),
        P(("ctx", "seg"), "head", None),
        P(("ctx", "seg"), "head", None),
        P("head", None, None),
        P("head", None, None),
        P(("ctx", "seg"), "head", None),
    )
    out_specs = P(("ctx", "seg"), "head", None)
    return jax.shard_map(
        on_device, mesh=mesh, in_specs=in_specs, out_specs=out_specs, check_vma=False
    )
```

profile of v0, /device:TPU:0, one launch (start us, length us, event | category | flops | bytes accessed | tf_op | source)
XLA Modules:
  0.0 226.0 jit_solution(13113540799511272979)
XLA Ops:
  8.5 2.1 fusion.86
  11.7 1.8 pad_maximum_fusion
  13.5 2.4 %collective-permute-start = (bf16[512,320]{1,0:T(8,128)(2,1)}, bf16[512,320]{1,0:T(8,128)(2,1)S(1)}, u32[]{:S(2)}, u32[]{:S(2)}) collective-permute-start(bf16[512,320]{1,0:T(8,128)(2,1)} %pad_maximum_fusion), channel_id=1, source_target_pairs={{0,1},{1,8},{8,9},{9,16},{16,17},{17,24},{24,25},{2,3},{3,10},{10,... | collective-permute-start | bytes 983048 | tf_op jit(solution)/shard_map/ppermute | solution.py:16
  16.2 15.6 %all_gather.6 = bf16[128,320]{1,0:T(8,128)(2,1)S(1)} all-gather(bf16[16,320]{1,0:T(8,128)(2,1)S(1)} %pad_maximum_fusion.1), channel_id=1, replica_groups=mesh['ctx'=4,'head'=4,'seg'=2] {'ctx','seg'}, dimensions={0}, use_global_device_ids=true | all-gather | bytes 92160 | tf_op jit(solution)/shard_map/all_gather | solution.py:66
  32.5 5.9 %reduce-scatter.2.cloned.1.call-done = f32[16,3,512]{2,0,1:T(8,128)} async-done(((f32[64,3,512]{2,0,1:T(8,128)}), f32[16,3,512]{2,0,1:T(8,128)}) %reduce-scatter.2.cloned.1.call-update) | async-done | bytes 98320 | tf_op jit(solution)/shard_map/reduce_scatter | solution.py:42
  39.4 15.5 %all-gather.2.cloned.1.call-done = bf16[4096,320]{1,0:T(8,128)(2,1)} async-done(((bf16[512,320]{1,0:T(8,128)(2,1)}), bf16[4096,320]{1,0:T(8,128)(2,1)}) %all-gather.2.cloned.1.call-update) | async-done | bytes 2621456 | tf_op jit(solution)/shard_map/all_gather | solution.py:72
  54.9 4.5 %gather_fusion = bf16[64,64,320]{2,1,0:T(8,128)(2,1)} fusion(bf16[64,64,320]{2,1,0:T(8,128)(2,1)} %bitcast.193, s32[1024]{0:T(1024)S(1)} %pad_clamp_fusion), kind=kCustom, calls=%fused_computation | custom fusion | bytes 5243136 | tf_op jit(solution)/shard_map/gather | solution.py:73
  59.4 159.2 %while.16 = (s32[]{:T(128)}, bf16[4,128,16,128]{3,2,1,0:T(8,128)(2,1)}, s32[4]{0:T(128)S(1)}, f32[16,3,512]{2,0,1:T(8,128)S(1)}, s32[]{:T(128)}, /*index=5*/bf16...) while((s32[]{:T(128)}, ...), condition=%wide.region_10.11_spmd.clone, body=%wide.region_3.10_spmd.clone.sunk | while | flops 2376428544 | bytes 36854732 | solution.py:103
  60.8 4.3 %fusion.126 = f32[640,128,16]{1,0,2:T(8,128)} fusion(bf16[512,16,192]{0,2,1:T(8,128)(2,1)} %get-tuple-element.459, s32[]{:T(128)S(6)} %select_n.150, bf16[1024,320]{0,1:T(8,128)(2,1)S(1)} %get-tuple-element.463, s32[]{:T(128)S(6)} %select_n.151), kind=kOutput, calls=%fused_computation.46.clone.1 | convolution fusion | flops 503316480 | bytes 6275080 | tf_op jit(solution)/shard_map/while/body/eval_jaxpr/rhd,kd->hrk/dot_general | solution.py:20
  65.4 8.3 %fusion.127 = (f32[16,128]{1,0:T(8,128)S(1)}, bf16[16,128,640]{1,2,0:T(8,128)(2,1)}) fusion(f32[640,128,16]{1,0,2:T(8,128)} %fusion.126, pred[128,640]{0,1:T(8,128)(4,1)S(1)} %compare_and_fusion.4), kind=kOutput, calls=%fused_computation.103.clone.1 | output fusion | flops 10486399 | bytes 7954432 | tf_op jit(solution)/shard_map/while/body/eval_jaxpr/sub | solution.py:25
  73.7 4.0 %fusion.128 = f32[128,16,128]{2,0,1:T(8,128)} fusion(bf16[16,128,640]{1,2,0:T(8,128)(2,1)} %get-tuple-element.405, f32[128,16]{0,1:T(8,128)S(1)} %maximum_bitcast_fusion.6, f32[128,16]{0,1:T(8,128)S(1)} %get-tuple-element.407, bf16[1024,320]{0,1:T(8,128)(2,1)S(1)} %get-tuple-element.463, s32[]{:T(128)S(6)} %select_n.151, s32[]{:T(128)S(6)} %add.284), kind=kOutput, calls=%fused_computation.36.clone.1 | convolution fusion | flops 336068608 | bytes 3850248 | tf_op jit(solution)/shard_map/while/body/eval_jaxpr/hrk,kv->rhv/dot_general | solution.py:28
  81.7 6.9 %fusion.129 = (f32[16,128]{1,0:T(8,128)S(1)}, bf16[16,128,1024]{1,2,0:T(8,128)(2,1)}) fusion(pred[128,1024]{0,1:T(8,128)(4,1)S(1)} %compare_and_fusion.5, bf16[512,16,192]{0,2,1:T(8,128)(2,1)} %get-tuple-element.459, s32[]{:T(128)S(6)} %select_n.150, bf16[1024,320]{1,0:T(8,128)(2,1)S(1)} %bitcast.187), kind=kOutput, calls=%fused_computation.104.clone.1 | convolution fusion | flops 817890304 | bytes 5775364 | tf_op jit(solution)/shard_map/while/body/eval_jaxpr/sub | solution.py:25
  88.5 5.4 %fusion.130 = f32[128,16,128]{2,0,1:T(8,128)} fusion(bf16[16,128,1024]{1,2,0:T(8,128)(2,1)} %get-tuple-element.408, f32[128,16]{0,1:T(8,128)S(1)} %maximum_bitcast_fusion.7, f32[128,16]{0,1:T(8,128)S(1)} %get-tuple-element.410, bf16[1024,320]{1,0:T(8,128)(2,1)S(1)} %bitcast.188), kind=kOutput, calls=%fused_computation.37.clone.1 | convolution fusion | flops 537395200 | bytes 5521408 | tf_op jit(solution)/shard_map/while/body/eval_jaxpr/hrk,kv->rhv/dot_general | solution.py:28
  95.9 2.1 fusion.132
  100.5 4.3 %fusion.126 = f32[640,128,16]{1,0,2:T(8,128)} fusion(bf16[512,16,192]{0,2,1:T(8,128)(2,1)} %get-tuple-element.459, s32[]{:T(128)S(6)} %select_n.150, bf16[1024,320]{0,1:T(8,128)(2,1)S(1)} %get-tuple-element.463, s32[]{:T(128)S(6)} %select_n.151), kind=kOutput, calls=%fused_computation.46.clone.1 | convolution fusion | flops 503316480 | bytes 6275080 | tf_op jit(solution)/shard_map/while/body/eval_jaxpr/rhd,kd->hrk/dot_general | solution.py:20
  105.1 8.3 %fusion.127 = (f32[16,128]{1,0:T(8,128)S(1)}, bf16[16,128,640]{1,2,0:T(8,128)(2,1)}) fusion(f32[640,128,16]{1,0,2:T(8,128)} %fusion.126, pred[128,640]{0,1:T(8,128)(4,1)S(1)} %compare_and_fusion.4), kind=kOutput, calls=%fused_computation.103.clone.1 | output fusion | flops 10486399 | bytes 7954432 | tf_op jit(solution)/shard_map/while/body/eval_jaxpr/sub | solution.py:25
  113.5 4.0 %fusion.128 = f32[128,16,128]{2,0,1:T(8,128)} fusion(bf16[16,128,640]{1,2,0:T(8,128)(2,1)} %get-tuple-element.405, f32[128,16]{0,1:T(8,128)S(1)} %maximum_bitcast_fusion.6, f32[128,16]{0,1:T(8,128)S(1)} %get-tuple-element.407, bf16[1024,320]{0,1:T(8,128)(2,1)S(1)} %get-tuple-element.463, s32[]{:T(128)S(6)} %select_n.151, s32[]{:T(128)S(6)} %add.284), kind=kOutput, calls=%fused_computation.36.clone.1 | convolution fusion | flops 336068608 | bytes 3850248 | tf_op jit(solution)/shard_map/while/body/eval_jaxpr/hrk,kv->rhv/dot_general | solution.py:28
  121.4 6.9 %fusion.129 = (f32[16,128]{1,0:T(8,128)S(1)}, bf16[16,128,1024]{1,2,0:T(8,128)(2,1)}) fusion(pred[128,1024]{0,1:T(8,128)(4,1)S(1)} %compare_and_fusion.5, bf16[512,16,192]{0,2,1:T(8,128)(2,1)} %get-tuple-element.459, s32[]{:T(128)S(6)} %select_n.150, bf16[1024,320]{1,0:T(8,128)(2,1)S(1)} %bitcast.187), kind=kOutput, calls=%fused_computation.104.clone.1 | convolution fusion | flops 817890304 | bytes 5775364 | tf_op jit(solution)/shard_map/while/body/eval_jaxpr/sub | solution.py:25
  128.3 5.4 %fusion.130 = f32[128,16,128]{2,0,1:T(8,128)} fusion(bf16[16,128,1024]{1,2,0:T(8,128)(2,1)} %get-tuple-element.408, f32[128,16]{0,1:T(8,128)S(1)} %maximum_bitcast_fusion.7, f32[128,16]{0,1:T(8,128)S(1)} %get-tuple-element.410, bf16[1024,320]{1,0:T(8,128)(2,1)S(1)} %bitcast.188), kind=kOutput, calls=%fused_computation.37.clone.1 | convolution fusion | flops 537395200 | bytes 5521408 | tf_op jit(solution)/shard_map/while/body/eval_jaxpr/hrk,kv->rhv/dot_general | solution.py:28
  135.7 2.1 fusion.132
  140.3 4.3 %fusion.126 = f32[640,128,16]{1,0,2:T(8,128)} fusion(bf16[512,16,192]{0,2,1:T(8,128)(2,1)} %get-tuple-element.459, s32[]{:T(128)S(6)} %select_n.150, bf16[1024,320]{0,1:T(8,128)(2,1)S(1)} %get-tuple-element.463, s32[]{:T(128)S(6)} %select_n.151), kind=kOutput, calls=%fused_computation.46.clone.1 | convolution fusion | flops 503316480 | bytes 6275080 | tf_op jit(solution)/shard_map/while/body/eval_jaxpr/rhd,kd->hrk/dot_general | solution.py:20
  144.9 8.3 %fusion.127 = (f32[16,128]{1,0:T(8,128)S(1)}, bf16[16,128,640]{1,2,0:T(8,128)(2,1)}) fusion(f32[640,128,16]{1,0,2:T(8,128)} %fusion.126, pred[128,640]{0,1:T(8,128)(4,1)S(1)} %compare_and_fusion.4), kind=kOutput, calls=%fused_computation.103.clone.1 | output fusion | flops 10486399 | bytes 7954432 | tf_op jit(solution)/shard_map/while/body/eval_jaxpr/sub | solution.py:25
  153.3 4.0 %fusion.128 = f32[128,16,128]{2,0,1:T(8,128)} fusion(bf16[16,128,640]{1,2,0:T(8,128)(2,1)} %get-tuple-element.405, f32[128,16]{0,1:T(8,128)S(1)} %maximum_bitcast_fusion.6, f32[128,16]{0,1:T(8,128)S(1)} %get-tuple-element.407, bf16[1024,320]{0,1:T(8,128)(2,1)S(1)} %get-tuple-element.463, s32[]{:T(128)S(6)} %select_n.151, s32[]{:T(128)S(6)} %add.284), kind=kOutput, calls=%fused_computation.36.clone.1 | convolution fusion | flops 336068608 | bytes 3850248 | tf_op jit(solution)/shard_map/while/body/eval_jaxpr/hrk,kv->rhv/dot_general | solution.py:28
  161.3 6.9 %fusion.129 = (f32[16,128]{1,0:T(8,128)S(1)}, bf16[16,128,1024]{1,2,0:T(8,128)(2,1)}) fusion(pred[128,1024]{0,1:T(8,128)(4,1)S(1)} %compare_and_fusion.5, bf16[512,16,192]{0,2,1:T(8,128)(2,1)} %get-tuple-element.459, s32[]{:T(128)S(6)} %select_n.150, bf16[1024,320]{1,0:T(8,128)(2,1)S(1)} %bitcast.187), kind=kOutput, calls=%fused_computation.104.clone.1 | convolution fusion | flops 817890304 | bytes 5775364 | tf_op jit(solution)/shard_map/while/body/eval_jaxpr/sub | solution.py:25
  168.1 5.4 %fusion.130 = f32[128,16,128]{2,0,1:T(8,128)} fusion(bf16[16,128,1024]{1,2,0:T(8,128)(2,1)} %get-tuple-element.408, f32[128,16]{0,1:T(8,128)S(1)} %maximum_bitcast_fusion.7, f32[128,16]{0,1:T(8,128)S(1)} %get-tuple-element.410, bf16[1024,320]{1,0:T(8,128)(2,1)S(1)} %bitcast.188), kind=kOutput, calls=%fused_computation.37.clone.1 | convolution fusion | flops 537395200 | bytes 5521408 | tf_op jit(solution)/shard_map/while/body/eval_jaxpr/hrk,kv->rhv/dot_general | solution.py:28
  175.5 2.1 fusion.132
  180.1 4.3 %fusion.126 = f32[640,128,16]{1,0,2:T(8,128)} fusion(bf16[512,16,192]{0,2,1:T(8,128)(2,1)} %get-tuple-element.459, s32[]{:T(128)S(6)} %select_n.150, bf16[1024,320]{0,1:T(8,128)(2,1)S(1)} %get-tuple-element.463, s32[]{:T(128)S(6)} %select_n.151), kind=kOutput, calls=%fused_computation.46.clone.1 | convolution fusion | flops 503316480 | bytes 6275080 | tf_op jit(solution)/shard_map/while/body/eval_jaxpr/rhd,kd->hrk/dot_general | solution.py:20
  184.8 8.3 %fusion.127 = (f32[16,128]{1,0:T(8,128)S(1)}, bf16[16,128,640]{1,2,0:T(8,128)(2,1)}) fusion(f32[640,128,16]{1,0,2:T(8,128)} %fusion.126, pred[128,640]{0,1:T(8,128)(4,1)S(1)} %compare_and_fusion.4), kind=kOutput, calls=%fused_computation.103.clone.1 | output fusion | flops 10486399 | bytes 7954432 | tf_op jit(solution)/shard_map/while/body/eval_jaxpr/sub | solution.py:25
  193.1 4.0 %fusion.128 = f32[128,16,128]{2,0,1:T(8,128)} fusion(bf16[16,128,640]{1,2,0:T(8,128)(2,1)} %get-tuple-element.405, f32[128,16]{0,1:T(8,128)S(1)} %maximum_bitcast_fusion.6, f32[128,16]{0,1:T(8,128)S(1)} %get-tuple-element.407, bf16[1024,320]{0,1:T(8,128)(2,1)S(1)} %get-tuple-element.463, s32[]{:T(128)S(6)} %select_n.151, s32[]{:T(128)S(6)} %add.284), kind=kOutput, calls=%fused_computation.36.clone.1 | convolution fusion | flops 336068608 | bytes 3850248 | tf_op jit(solution)/shard_map/while/body/eval_jaxpr/hrk,kv->rhv/dot_general | solution.py:28
  201.1 6.9 %fusion.129 = (f32[16,128]{1,0:T(8,128)S(1)}, bf16[16,128,1024]{1,2,0:T(8,128)(2,1)}) fusion(pred[128,1024]{0,1:T(8,128)(4,1)S(1)} %compare_and_fusion.5, bf16[512,16,192]{0,2,1:T(8,128)(2,1)} %get-tuple-element.459, s32[]{:T(128)S(6)} %select_n.150, bf16[1024,320]{1,0:T(8,128)(2,1)S(1)} %bitcast.187), kind=kOutput, calls=%fused_computation.104.clone.1 | convolution fusion | flops 817890304 | bytes 5775364 | tf_op jit(solution)/shard_map/while/body/eval_jaxpr/sub | solution.py:25
  207.9 5.4 %fusion.130 = f32[128,16,128]{2,0,1:T(8,128)} fusion(bf16[16,128,1024]{1,2,0:T(8,128)(2,1)} %get-tuple-element.408, f32[128,16]{0,1:T(8,128)S(1)} %maximum_bitcast_fusion.7, f32[128,16]{0,1:T(8,128)S(1)} %get-tuple-element.410, bf16[1024,320]{1,0:T(8,128)(2,1)S(1)} %bitcast.188), kind=kOutput, calls=%fused_computation.37.clone.1 | convolution fusion | flops 537395200 | bytes 5521408 | tf_op jit(solution)/shard_map/while/body/eval_jaxpr/hrk,kv->rhv/dot_general | solution.py:28
  215.3 2.1 fusion.132
  (118 shorter events, 27.6 us)
Async XLA Ops:
  7.4 1.1 copy-start
  7.4 8.6 %copy-start.1 = (bf16[512,1,128]{2,0,1:T(8,128)(2,1)S(1)}, bf16[512,1,128]{2,0,1:T(8,128)(2,1)}, u32[]{:S(2)}) copy-start(bf16[512,1,128]{2,0,1:T(8,128)(2,1)} %param.14) | copy-start | bytes 393220
  7.4 8.6 %copy-start.3 = (bf16[1,32,128]{2,1,0:T(8,128)(2,1)S(1)}, bf16[1,32,128]{2,1,0:T(8,128)(2,1)}, u32[]{:S(2)}) copy-start(bf16[1,32,128]{2,1,0:T(8,128)(2,1)} %param.16) | copy-start | bytes 24580
  7.4 8.7 %copy-start.2 = (bf16[1,32,192]{2,1,0:T(8,128)(2,1)S(1)}, bf16[1,32,192]{2,1,0:T(8,128)(2,1)}, u32[]{:S(2)}) copy-start(bf16[1,32,192]{2,1,0:T(8,128)(2,1)} %param.15) | copy-start | bytes 36868
  7.4 24.6 %copy-start.4 = (s32[4,1,16]{2,1,0:T(1,128)S(1)}, s32[4,1,16]{2,1,0:T(1,128)}, u32[]{:S(2)}) copy-start(s32[4,1,16]{2,1,0:T(1,128)} %param.17) | copy-start | bytes 772
  7.4 31.1 %reduce-scatter.2.cloned.1.call-start = ((), (), s32[]{:S(2)}) async-start(), calls=%async_computation.1 | async-start | bytes 491520 | tf_op jit(solution)/shard_map/reduce_scatter | solution.py:42
  10.6 44.3 %all-gather.2.cloned.1.call-start = ((), (), s32[]{:S(2)}) async-start(), calls=%async_computation.2 | async-start | bytes 3538944 | tf_op jit(solution)/shard_map/all_gather | solution.py:72
  13.5 18.6 %collective-permute-start = (bf16[512,320]{1,0:T(8,128)(2,1)}, bf16[512,320]{1,0:T(8,128)(2,1)S(1)}, u32[]{:S(2)}, u32[]{:S(2)}) collective-permute-start(bf16[512,320]{1,0:T(8,128)(2,1)} %pad_maximum_fusion), channel_id=1, source_target_pairs={{0,1},{1,8},{8,9},{9,16},{16,17},{17,24},{24,25},{2,3},{3,10},{10,... | collective-permute-start | bytes 983048 | tf_op jit(solution)/shard_map/ppermute | solution.py:16
Sparse Core Ops, SparseCore 0:
  11.0 27.4 reduce-scatter.1
Sparse Core Ops, SparseCore 1:
  13.6 41.2 all-gather.1
where the time goes:
time: 228 us; the launch traced here: 226 us
  matrix products  100 us (44%)
  other arithmetic  39.5 us (17%)
  waiting for transfers between devices  21.5 us (9%)
  local copies, waits for them, and re-layouts  20.6 us (9%)
  blocking collectives  15.6 us (7%)
  between operations  15 us (7%)
  loops' own time  11.2 us (5%)
  starting transfers between devices  2.5 us (1%)
    dot_general x12, matrix products, attend(): jnp.einsum('hrk,kv->rhv', rounded, values_part, preferred_element_type=jn...  46.3 us
    sub x8, matrix products, attend(): weights = jnp.where(allowed[None], jnp.exp(scores - highest), 0.0)  34.5 us
    sub x4, other arithmetic, attend(): weights = jnp.where(allowed[None], jnp.exp(scores - highest), 0.0)  33.2 us
    dot_general x4, matrix products, attend(): jnp.einsum('rhd,kd->hrk', query, keys_part, preferred_element_type=jnp.fl...  17.4 us
    all_gather x1, blocking collectives, on_device(): coarse = lax.all_gather(coarse_packed, ('ctx', 'seg'), axis=0, tiled=True)  15.6 us
    all_gather x1, waiting for transfers between devices, on_device(): everything = lax.all_gather(packed, ('ctx', 'seg'), axis=0, tiled=True)  15.5 us
    another operation x1, loops' own time, on_device(): tiles = lax.map(one_tile, jnp.arange(local_count // TILE, dtype=jnp.int32))  11.2 us
    reduce_scatter x1, waiting for transfers between devices, on_device(): lax.psum_scatter(jnp.einsum('hcd,td->hct', rows, tokens_x, preferred_elem...  5.93 us
  transfers between devices with their start and end apart: 3, of which 2 were waited for; matrix products, arithmetic and copies ran while one was open for 2% of the time, Pallas kernels for 0%

commit v1 on v0

--- a/solution.py
+++ b/solution.py
@@ -69,7 +69,10 @@
     extended = jnp.concatenate([previous, packed], axis=0)
     chosen_all = selected[:, 0, :]
     blocks_all = jnp.maximum(chosen_all, 0)
-    everything = lax.all_gather(packed, ("ctx", "seg"), axis=0, tiled=True)
+    size = lax.axis_size(("ctx", "seg"))
+    pieces = jnp.stack([packed for _ in range(size)])
+    pieces = lax.all_to_all(pieces, ("ctx", "seg"), split_axis=0, concat_axis=0)
+    everything = jnp.concatenate(pieces, axis=0)
     picked = everything.reshape(-1, BLK_S, packed.shape[1])[blocks_all]
 
     def one_tile(tile):

time: 228 us -> 270 us (1.18)
  blocking collectives: 15.6 us -> 61.1 us
  waiting for transfers between devices: 21.5 us -> 0.02 us
  starting transfers between devices: 2.5 us -> 9.63 us
  local copies, waits for them, and re-layouts: 20.6 us -> 27.6 us
  other arithmetic: 39.5 us -> 44.8 us
    all_gather x1, blocking collectives: 15.6 us -> 61.1 us  [on_device(): coarse = lax.all_gather(coarse_packed, ('ctx', 'seg'), axis=0, tiled=True)]
    all_gather x1 -> x0, waiting for transfers between devices: 15.5 us -> none  [on_device(): everything = lax.all_gather(packed, ('ctx', 'seg'), axis=0, tiled=True)]
    all_to_all x0 -> x1, starting transfers between devices: none -> 6.5 us  [on_device(): pieces = lax.all_to_all(pieces, ('ctx', 'seg'), split_axis=0, concat_axis=0)]
    reduce_scatter x1, waiting for transfers between devices: 5.93 us -> 0.01 us  [on_device(): lax.psum_scatter(jnp.einsum('hcd,td->hct', rows, tokens_x, preferred_elem...]
    all_to_all x0 -> x1, local copies, waits for them, and re-layouts: none -> 2.79 us  [on_device(): pieces = lax.all_to_all(pieces, ('ctx', 'seg'), split_axis=0, concat_axis=0)]
  transfers between devices with their start and end apart: 3 -> 3, of which waited for: 2 -> 0; matrix products, arithmetic and copies ran while one was open for 2% -> 5% of each run, Pallas kernels for 0% -> 0%
where the time goes in v1:
time: 270 us; the launch traced here: 268 us
  matrix products  100 us (37%)
  blocking collectives  61.1 us (23%)
  other arithmetic  44.8 us (17%)
  local copies, waits for them, and re-layouts  27.6 us (10%)
  between operations  13.5 us (5%)
  loops' own time  11.4 us (4%)
  starting transfers between devices  9.63 us (4%)
    all_gather x1, blocking collectives, on_device(): coarse = lax.all_gather(coarse_packed, ('ctx', 'seg'), axis=0, tiled=True)  61.1 us
    dot_general x12, matrix products, attend(): jnp.einsum('hrk,kv->rhv', rounded, values_part, preferred_element_type=jn...  46.3 us
    sub x8, matrix products, attend(): weights = jnp.where(allowed[None], jnp.exp(scores - highest), 0.0)  34.5 us
    sub x4, other arithmetic, attend(): weights = jnp.where(allowed[None], jnp.exp(scores - highest), 0.0)  33.2 us
    dot_general x4, matrix products, attend(): jnp.einsum('rhd,kd->hrk', query, keys_part, preferred_element_type=jnp.fl...  17.4 us
    another operation x1, loops' own time, on_device(): tiles = lax.map(one_tile, jnp.arange(local_count // TILE, dtype=jnp.int32))  11.4 us
    all_to_all x1, starting transfers between devices, on_device(): pieces = lax.all_to_all(pieces, ('ctx', 'seg'), split_axis=0, concat_axis=0)  6.5 us
  transfers between devices with their start and end apart: 3, of which 0 were waited for; matrix products, arithmetic and copies ran while one was open for 5% of the time, Pallas kernels for 0%

profile of v1, /device:TPU:0, one launch (start us, length us, event | category | flops | bytes accessed | tf_op | source)
XLA Modules:
  0.0 268.3 jit_solution(8002712552296288936)
XLA Ops:
  11.1 6.5 %all-to-all-start = ((bf16[8,512,320]{1,2,0:T(8,128)(2,1)}), bf16[8,512,320]{1,2,0:T(8,128)(2,1)S(1)}, u32[]{:S(2)}, u32[]{:S(2)}) async-start(bf16[8,512,320]{1,2,0:T(8,128)(2,1)} %stack.2), calls=%async_computation.1 | async-start | bytes 5242880 | tf_op jit(solution)/shard_map/all_to_all | solution.py:74
  17.6 3.1 %collective-permute-start = (bf16[512,320]{0,1:T(8,128)(2,1)}, bf16[512,320]{0,1:T(8,128)(2,1)}, u32[]{:S(2)}, u32[]{:S(2)}) collective-permute-start(bf16[512,320]{0,1:T(8,128)(2,1)} %copy-done.3), channel_id=1, source_target_pairs={{0,1},{1,8},{8,9},{9,16},{16,17},{17,24},{24,25},{2,3},{3,10},{10,... | collective-permute-start | bytes 983048 | tf_op jit(solution)/shard_map/ppermute | solution.py:16
  20.7 2.1 fusion.86
  25.8 61.1 %all_gather.3 = bf16[128,320]{1,0:T(8,128)(2,1)} all-gather(bf16[16,320]{1,0:T(8,128)(2,1)S(1)} %pad_maximum_fusion.1), channel_id=1, replica_groups=mesh['ctx'=4,'head'=4,'seg'=2] {'ctx','seg'}, dimensions={0}, use_global_device_ids=true | all-gather | bytes 92160 | tf_op jit(solution)/shard_map/all_gather | solution.py:66
  91.7 2.0 maximum_maximum_fusion
  94.6 2.8 %copy.53 = bf16[8,512,320]{2,1,0:T(8,128)(2,1)} copy(bf16[8,512,320]{1,2,0:T(8,128)(2,1)S(1)} %all-to-all-done) | data formatting | bytes 5242880 | tf_op jit(solution)/shard_map/all_to_all | solution.py:74
  97.4 4.6 %gather_fusion = bf16[64,64,320]{2,1,0:T(8,128)(2,1)} fusion(bf16[64,64,320]{2,1,0:T(8,128)(2,1)} %bitcast.190, s32[1024]{0:T(1024)S(1)} %copy-done.6), kind=kCustom, calls=%fused_computation | custom fusion | bytes 5243136 | tf_op jit(solution)/shard_map/gather | solution.py:76
  102.0 159.4 %while.16 = (s32[]{:T(128)}, bf16[4,128,16,128]{3,2,1,0:T(8,128)(2,1)}, s32[4]{0:T(128)S(1)}, f32[16,3,512]{2,0,1:T(8,128)S(1)}, s32[]{:T(128)}, /*index=5*/bf16...) while((s32[]{:T(128)}, ...), condition=%wide.region_10.11_spmd.clone, body=%wide.region_3.10_spmd.clone.sunk | while | flops 2376428544 | bytes 36854732 | solution.py:106
  103.6 4.3 %fusion.126 = f32[640,128,16]{1,0,2:T(8,128)} fusion(bf16[512,16,192]{0,2,1:T(8,128)(2,1)} %get-tuple-element.459, s32[]{:T(128)S(6)} %select_n.150, bf16[1024,320]{0,1:T(8,128)(2,1)S(1)} %get-tuple-element.463, s32[]{:T(128)S(6)} %select_n.151), kind=kOutput, calls=%fused_computation.46.clone.1 | convolution fusion | flops 503316480 | bytes 6275080 | tf_op jit(solution)/shard_map/while/body/eval_jaxpr/rhd,kd->hrk/dot_general | solution.py:20
  108.2 8.3 %fusion.127 = (f32[16,128]{1,0:T(8,128)S(1)}, bf16[16,128,640]{1,2,0:T(8,128)(2,1)}) fusion(f32[640,128,16]{1,0,2:T(8,128)} %fusion.126, pred[128,640]{0,1:T(8,128)(4,1)S(1)} %compare_and_fusion.4), kind=kOutput, calls=%fused_computation.103.clone.1 | output fusion | flops 10486399 | bytes 7954432 | tf_op jit(solution)/shard_map/while/body/eval_jaxpr/sub | solution.py:25
  116.5 4.0 %fusion.128 = f32[128,16,128]{2,0,1:T(8,128)} fusion(bf16[16,128,640]{1,2,0:T(8,128)(2,1)} %get-tuple-element.405, f32[128,16]{0,1:T(8,128)S(1)} %maximum_bitcast_fusion.6, f32[128,16]{0,1:T(8,128)S(1)} %get-tuple-element.407, bf16[1024,320]{0,1:T(8,128)(2,1)S(1)} %get-tuple-element.463, s32[]{:T(128)S(6)} %select_n.151, s32[]{:T(128)S(6)} %add.284), kind=kOutput, calls=%fused_computation.36.clone.1 | convolution fusion | flops 336068608 | bytes 3850248 | tf_op jit(solution)/shard_map/while/body/eval_jaxpr/hrk,kv->rhv/dot_general | solution.py:28
  124.5 6.9 %fusion.129 = (f32[16,128]{1,0:T(8,128)S(1)}, bf16[16,128,1024]{1,2,0:T(8,128)(2,1)}) fusion(pred[128,1024]{0,1:T(8,128)(4,1)S(1)} %compare_and_fusion.5, bf16[512,16,192]{0,2,1:T(8,128)(2,1)} %get-tuple-element.459, s32[]{:T(128)S(6)} %select_n.150, bf16[1024,320]{1,0:T(8,128)(2,1)S(1)} %bitcast.187), kind=kOutput, calls=%fused_computation.104.clone.1 | convolution fusion | flops 817890304 | bytes 5775364 | tf_op jit(solution)/shard_map/while/body/eval_jaxpr/sub | solution.py:25
  131.3 5.4 %fusion.130 = f32[128,16,128]{2,0,1:T(8,128)} fusion(bf16[16,128,1024]{1,2,0:T(8,128)(2,1)} %get-tuple-element.408, f32[128,16]{0,1:T(8,128)S(1)} %maximum_bitcast_fusion.7, f32[128,16]{0,1:T(8,128)S(1)} %get-tuple-element.410, bf16[1024,320]{1,0:T(8,128)(2,1)S(1)} %bitcast.188), kind=kOutput, calls=%fused_computation.37.clone.1 | convolution fusion | flops 537395200 | bytes 5521408 | tf_op jit(solution)/shard_map/while/body/eval_jaxpr/hrk,kv->rhv/dot_general | solution.py:28
  138.7 2.1 fusion.132
  143.4 4.3 %fusion.126 = f32[640,128,16]{1,0,2:T(8,128)} fusion(bf16[512,16,192]{0,2,1:T(8,128)(2,1)} %get-tuple-element.459, s32[]{:T(128)S(6)} %select_n.150, bf16[1024,320]{0,1:T(8,128)(2,1)S(1)} %get-tuple-element.463, s32[]{:T(128)S(6)} %select_n.151), kind=kOutput, calls=%fused_computation.46.clone.1 | convolution fusion | flops 503316480 | bytes 6275080 | tf_op jit(solution)/shard_map/while/body/eval_jaxpr/rhd,kd->hrk/dot_general | solution.py:20
  148.0 8.3 %fusion.127 = (f32[16,128]{1,0:T(8,128)S(1)}, bf16[16,128,640]{1,2,0:T(8,128)(2,1)}) fusion(f32[640,128,16]{1,0,2:T(8,128)} %fusion.126, pred[128,640]{0,1:T(8,128)(4,1)S(1)} %compare_and_fusion.4), kind=kOutput, calls=%fused_computation.103.clone.1 | output fusion | flops 10486399 | bytes 7954432 | tf_op jit(solution)/shard_map/while/body/eval_jaxpr/sub | solution.py:25
  156.3 4.0 %fusion.128 = f32[128,16,128]{2,0,1:T(8,128)} fusion(bf16[16,128,640]{1,2,0:T(8,128)(2,1)} %get-tuple-element.405, f32[128,16]{0,1:T(8,128)S(1)} %maximum_bitcast_fusion.6, f32[128,16]{0,1:T(8,128)S(1)} %get-tuple-element.407, bf16[1024,320]{0,1:T(8,128)(2,1)S(1)} %get-tuple-element.463, s32[]{:T(128)S(6)} %select_n.151, s32[]{:T(128)S(6)} %add.284), kind=kOutput, calls=%fused_computation.36.clone.1 | convolution fusion | flops 336068608 | bytes 3850248 | tf_op jit(solution)/shard_map/while/body/eval_jaxpr/hrk,kv->rhv/dot_general | solution.py:28
  164.3 6.9 %fusion.129 = (f32[16,128]{1,0:T(8,128)S(1)}, bf16[16,128,1024]{1,2,0:T(8,128)(2,1)}) fusion(pred[128,1024]{0,1:T(8,128)(4,1)S(1)} %compare_and_fusion.5, bf16[512,16,192]{0,2,1:T(8,128)(2,1)} %get-tuple-element.459, s32[]{:T(128)S(6)} %select_n.150, bf16[1024,320]{1,0:T(8,128)(2,1)S(1)} %bitcast.187), kind=kOutput, calls=%fused_computation.104.clone.1 | convolution fusion | flops 817890304 | bytes 5775364 | tf_op jit(solution)/shard_map/while/body/eval_jaxpr/sub | solution.py:25
  171.1 5.4 %fusion.130 = f32[128,16,128]{2,0,1:T(8,128)} fusion(bf16[16,128,1024]{1,2,0:T(8,128)(2,1)} %get-tuple-element.408, f32[128,16]{0,1:T(8,128)S(1)} %maximum_bitcast_fusion.7, f32[128,16]{0,1:T(8,128)S(1)} %get-tuple-element.410, bf16[1024,320]{1,0:T(8,128)(2,1)S(1)} %bitcast.188), kind=kOutput, calls=%fused_computation.37.clone.1 | convolution fusion | flops 537395200 | bytes 5521408 | tf_op jit(solution)/shard_map/while/body/eval_jaxpr/hrk,kv->rhv/dot_general | solution.py:28
  178.5 2.1 fusion.132
  183.1 4.3 %fusion.126 = f32[640,128,16]{1,0,2:T(8,128)} fusion(bf16[512,16,192]{0,2,1:T(8,128)(2,1)} %get-tuple-element.459, s32[]{:T(128)S(6)} %select_n.150, bf16[1024,320]{0,1:T(8,128)(2,1)S(1)} %get-tuple-element.463, s32[]{:T(128)S(6)} %select_n.151), kind=kOutput, calls=%fused_computation.46.clone.1 | convolution fusion | flops 503316480 | bytes 6275080 | tf_op jit(solution)/shard_map/while/body/eval_jaxpr/rhd,kd->hrk/dot_general | solution.py:20
  187.7 8.3 %fusion.127 = (f32[16,128]{1,0:T(8,128)S(1)}, bf16[16,128,640]{1,2,0:T(8,128)(2,1)}) fusion(f32[640,128,16]{1,0,2:T(8,128)} %fusion.126, pred[128,640]{0,1:T(8,128)(4,1)S(1)} %compare_and_fusion.4), kind=kOutput, calls=%fused_computation.103.clone.1 | output fusion | flops 10486399 | bytes 7954432 | tf_op jit(solution)/shard_map/while/body/eval_jaxpr/sub | solution.py:25
  196.1 4.0 %fusion.128 = f32[128,16,128]{2,0,1:T(8,128)} fusion(bf16[16,128,640]{1,2,0:T(8,128)(2,1)} %get-tuple-element.405, f32[128,16]{0,1:T(8,128)S(1)} %maximum_bitcast_fusion.6, f32[128,16]{0,1:T(8,128)S(1)} %get-tuple-element.407, bf16[1024,320]{0,1:T(8,128)(2,1)S(1)} %get-tuple-element.463, s32[]{:T(128)S(6)} %select_n.151, s32[]{:T(128)S(6)} %add.284), kind=kOutput, calls=%fused_computation.36.clone.1 | convolution fusion | flops 336068608 | bytes 3850248 | tf_op jit(solution)/shard_map/while/body/eval_jaxpr/hrk,kv->rhv/dot_general | solution.py:28
  204.1 6.9 %fusion.129 = (f32[16,128]{1,0:T(8,128)S(1)}, bf16[16,128,1024]{1,2,0:T(8,128)(2,1)}) fusion(pred[128,1024]{0,1:T(8,128)(4,1)S(1)} %compare_and_fusion.5, bf16[512,16,192]{0,2,1:T(8,128)(2,1)} %get-tuple-element.459, s32[]{:T(128)S(6)} %select_n.150, bf16[1024,320]{1,0:T(8,128)(2,1)S(1)} %bitcast.187), kind=kOutput, calls=%fused_computation.104.clone.1 | convolution fusion | flops 817890304 | bytes 5775364 | tf_op jit(solution)/shard_map/while/body/eval_jaxpr/sub | solution.py:25
  210.9 5.4 %fusion.130 = f32[128,16,128]{2,0,1:T(8,128)} fusion(bf16[16,128,1024]{1,2,0:T(8,128)(2,1)} %get-tuple-element.408, f32[128,16]{0,1:T(8,128)S(1)} %maximum_bitcast_fusion.7, f32[128,16]{0,1:T(8,128)S(1)} %get-tuple-element.410, bf16[1024,320]{1,0:T(8,128)(2,1)S(1)} %bitcast.188), kind=kOutput, calls=%fused_computation.37.clone.1 | convolution fusion | flops 537395200 | bytes 5521408 | tf_op jit(solution)/shard_map/while/body/eval_jaxpr/hrk,kv->rhv/dot_general | solution.py:28
  218.3 2.1 fusion.132
  222.9 4.3 %fusion.126 = f32[640,128,16]{1,0,2:T(8,128)} fusion(bf16[512,16,192]{0,2,1:T(8,128)(2,1)} %get-tuple-element.459, s32[]{:T(128)S(6)} %select_n.150, bf16[1024,320]{0,1:T(8,128)(2,1)S(1)} %get-tuple-element.463, s32[]{:T(128)S(6)} %select_n.151), kind=kOutput, calls=%fused_computation.46.clone.1 | convolution fusion | flops 503316480 | bytes 6275080 | tf_op jit(solution)/shard_map/while/body/eval_jaxpr/rhd,kd->hrk/dot_general | solution.py:20
  227.6 8.3 %fusion.127 = (f32[16,128]{1,0:T(8,128)S(1)}, bf16[16,128,640]{1,2,0:T(8,128)(2,1)}) fusion(f32[640,128,16]{1,0,2:T(8,128)} %fusion.126, pred[128,640]{0,1:T(8,128)(4,1)S(1)} %compare_and_fusion.4), kind=kOutput, calls=%fused_computation.103.clone.1 | output fusion | flops 10486399 | bytes 7954432 | tf_op jit(solution)/shard_map/while/body/eval_jaxpr/sub | solution.py:25
  235.9 4.0 %fusion.128 = f32[128,16,128]{2,0,1:T(8,128)} fusion(bf16[16,128,640]{1,2,0:T(8,128)(2,1)} %get-tuple-element.405, f32[128,16]{0,1:T(8,128)S(1)} %maximum_bitcast_fusion.6, f32[128,16]{0,1:T(8,128)S(1)} %get-tuple-element.407, bf16[1024,320]{0,1:T(8,128)(2,1)S(1)} %get-tuple-element.463, s32[]{:T(128)S(6)} %select_n.151, s32[]{:T(128)S(6)} %add.284), kind=kOutput, calls=%fused_computation.36.clone.1 | convolution fusion | flops 336068608 | bytes 3850248 | tf_op jit(solution)/shard_map/while/body/eval_jaxpr/hrk,kv->rhv/dot_general | solution.py:28
  243.9 6.9 %fusion.129 = (f32[16,128]{1,0:T(8,128)S(1)}, bf16[16,128,1024]{1,2,0:T(8,128)(2,1)}) fusion(pred[128,1024]{0,1:T(8,128)(4,1)S(1)} %compare_and_fusion.5, bf16[512,16,192]{0,2,1:T(8,128)(2,1)} %get-tuple-element.459, s32[]{:T(128)S(6)} %select_n.150, bf16[1024,320]{1,0:T(8,128)(2,1)S(1)} %bitcast.187), kind=kOutput, calls=%fused_computation.104.clone.1 | convolution fusion | flops 817890304 | bytes 5775364 | tf_op jit(solution)/shard_map/while/body/eval_jaxpr/sub | solution.py:25
  250.7 5.4 %fusion.130 = f32[128,16,128]{2,0,1:T(8,128)} fusion(bf16[16,128,1024]{1,2,0:T(8,128)(2,1)} %get-tuple-element.408, f32[128,16]{0,1:T(8,128)S(1)} %maximum_bitcast_fusion.7, f32[128,16]{0,1:T(8,128)S(1)} %get-tuple-element.410, bf16[1024,320]{1,0:T(8,128)(2,1)S(1)} %bitcast.188), kind=kOutput, calls=%fused_computation.37.clone.1 | convolution fusion | flops 537395200 | bytes 5521408 | tf_op jit(solution)/shard_map/while/body/eval_jaxpr/hrk,kv->rhv/dot_general | solution.py:28
  258.1 2.1 fusion.132
  (127 shorter events, 36.9 us)
Async XLA Ops:
  6.5 14.2 %copy-start = (bf16[512,640]{1,0:T(8,128)(2,1)S(1)}, bf16[512,640]{1,0:T(8,128)(2,1)}, u32[]{:S(2)}) copy-start(bf16[512,640]{1,0:T(8,128)(2,1)} %param.10) | copy-start | bytes 1966084
  7.6 3.5 %copy-start.4 = (bf16[512,1,128]{0,2,1:T(8,128)(2,1)}, bf16[512,1,128]{0,2,1:T(8,128)(2,1)S(1)}, u32[]{:S(2)}) copy-start(bf16[512,1,128]{0,2,1:T(8,128)(2,1)S(1)} %copy.52) | copy-start | bytes 393220
  8.6 0.7 copy-start.3
  11.1 11.7 %copy-start.5 = (bf16[1,32,192]{2,1,0:T(8,128)(2,1)S(1)}, bf16[1,32,192]{2,1,0:T(8,128)(2,1)}, u32[]{:S(2)}) copy-start(bf16[1,32,192]{2,1,0:T(8,128)(2,1)} %param.15) | copy-start | bytes 36868
  11.1 11.8 %copy-start.7 = (bf16[1,32,128]{2,1,0:T(8,128)(2,1)S(1)}, bf16[1,32,128]{2,1,0:T(8,128)(2,1)}, u32[]{:S(2)}) copy-start(bf16[1,32,128]{2,1,0:T(8,128)(2,1)} %param.16) | copy-start | bytes 24580
  11.1 11.8 %copy-start.2 = (bf16[512,1,192]{0,2,1:T(8,128)(2,1)S(1)}, bf16[512,1,192]{0,2,1:T(8,128)(2,1)}, u32[]{:S(2)}) copy-start(bf16[512,1,192]{0,2,1:T(8,128)(2,1)} %param.13) | copy-start | bytes 589828
  11.1 83.5 %all-to-all-start = ((bf16[8,512,320]{1,2,0:T(8,128)(2,1)}), bf16[8,512,320]{1,2,0:T(8,128)(2,1)S(1)}, u32[]{:S(2)}, u32[]{:S(2)}) async-start(bf16[8,512,320]{1,2,0:T(8,128)(2,1)} %stack.2), calls=%async_computation.1 | async-start | bytes 5242880 | tf_op jit(solution)/shard_map/all_to_all | solution.py:74
  17.6 76.1 %reduce-scatter.2.cloned.1.call-start = ((), (), s32[]{:S(2)}) async-start(), calls=%async_computation.2 | async-start | bytes 491520 | tf_op jit(solution)/shard_map/reduce_scatter | solution.py:42
  17.6 74.1 %collective-permute-start = (bf16[512,320]{0,1:T(8,128)(2,1)}, bf16[512,320]{0,1:T(8,128)(2,1)}, u32[]{:S(2)}, u32[]{:S(2)}) collective-permute-start(bf16[512,320]{0,1:T(8,128)(2,1)} %copy-done.3), channel_id=1, source_target_pairs={{0,1},{1,8},{8,9},{9,16},{16,17},{17,24},{24,25},{2,3},{3,10},{10,... | collective-permute-start | bytes 983048 | tf_op jit(solution)/shard_map/ppermute | solution.py:16
  93.7 3.7 %copy-start.6 = (s32[1024]{0:T(1024)S(1)}, s32[1024]{0:T(1024)}, u32[]{:S(2)}) copy-start(s32[1024]{0:T(1024)} %pad_clamp_fusion) | copy-start | bytes 12292
  97.4 4.6 %copy-start.1 = (bf16[1024,320]{0,1:T(8,128)(2,1)S(1)}, bf16[1024,320]{0,1:T(8,128)(2,1)}, u32[]{:S(2)}) copy-start(bf16[1024,320]{0,1:T(8,128)(2,1)} %maximum_maximum_fusion) | copy-start | bytes 1966084
  97.4 4.6 %copy-start.8 = (s32[4,1,16]{2,1,0:T(1,128)S(1)}, s32[4,1,16]{2,1,0:T(1,128)}, u32[]{:S(2)}) copy-start(s32[4,1,16]{2,1,0:T(1,128)} %param.17) | copy-start | bytes 772
Sparse Core Ops, SparseCore 0:
  23.0 25.2 reduce-scatter.1
